TPU v7x, 512 devices: a whole 4x4x16 slice. The times are simulated.
512 devices in a mesh: dim: 16 (over z_hi, y, core), row: 32 (over x, z_lo).
Axes of the slice: x: 4, y: 4, z: 16 (z_hi: 2, z_lo: 8; z = z_hi * 8 + z_lo), core: 2. Of those that a mesh axis runs over, the one named last changes fastest.
Arguments:
- vectors: bfloat16 [53248, 4096], P('row', 'dim'), may hold values from -6 to 6
- blocks: float32 [5, 4096, 128], P(None, 'dim'), may hold values from -0.5 to 0.5
- angles: float32 [5, 4096], P(None, 'dim'), may hold values from -3.140625 to 3.140625
- codes: int32 [53248, 4096], P('row', 'dim'), may hold values from 0 to 15
- scale_index: int32 [53248], P('row'), may hold values from 0 to 15
- scale_table: float32 [16], replicated, may hold values from 0.05 to 0.3
- block_state: float32 [5, 4096, 128], P(None, 'dim'), may hold values from 0.1 to 2
- angle_state: float32 [5, 4096], P(None, 'dim'), may hold values from 0.1 to 2
Outputs:
- step_blocks: float32 [5, 4096, 128], P(None, 'dim')
- new_block_state: float32 [5, 4096, 128], P(None, 'dim')
- step_angles: float32 [5, 4096], P(None, 'dim')
- new_angle_state: float32 [5, 4096], P(None, 'dim')
All inputs are finite; a program needn't handle non-finite values.
Results may differ from a plain program's by a relative error of at most 0.015.
The roundings to bfloat16 on the way count: a program that leaves them out, or rounds other values in their place, can miss the bound.
Values may be sent and summed in bfloat16 or wider, within the bound.
A program may use at most 128 MiB of HBM per device.

v0:
```python
import math

import jax
import jax.numpy as jnp
from jax import lax
from jax.sharding import PartitionSpec as P

BLOCK = 128
S = 5


def swapped(value, axis, distance):
    mask = 2**distance
    pairs = [(source, source ^ mask) for source in range(lax.axis_size(axis))]
    return lax.ppermute(value, axis, pairs)


def swap_halves(tensor, section):
    layout = tensor.shape
    stride = 2**section
    number = layout[-2]
    parted = tensor.reshape(layout[:-2] + (number // (2 * stride), 2, stride, layout[-1]))
    return jnp.flip(parted, axis=-3).reshape(layout)


def local(vectors, blocks, angles, codes, scale_index, scale_table, block_state, angle_state):
    num_rows = vectors.shape[0]
    width = vectors.shape[1]
    local_blocks = width // BLOCK
    local_bits = local_blocks.bit_length() - 1
    device = lax.axis_index("dim")
    global_ids = device * local_blocks + jnp.arange(local_blocks, dtype=jnp.int32)
    weights = blocks.astype(jnp.bfloat16).reshape(S, local_blocks, BLOCK, BLOCK)
    thetas = angles.reshape(S, local_blocks, BLOCK)
    cosines = jnp.cos(thetas)
    sines = jnp.sin(thetas)
    current = vectors.reshape(num_rows, local_blocks, BLOCK)
    saved = []
    for section in range(S):
        signs = jnp.where(global_ids // 2**section % 2 == 0, 1.0, -1.0).astype(jnp.float32)[:, None]
        mixed = jnp.einsum(
            "rnb,nbc->rnc", current, weights[section], preferred_element_type=jnp.float32
        ).astype(jnp.bfloat16)
        if section < local_bits:
            partner = swap_halves(mixed, section)
        else:
            partner = swapped(mixed, "dim", section - local_bits)
        result = (
            cosines[section] * mixed.astype(jnp.float32)
            + signs * sines[section] * partner.astype(jnp.float32)
        ).astype(jnp.bfloat16)
        saved.append((current, mixed, partner, signs))
        current = result
    levels = (
        scale_index[:, None] == jnp.arange(scale_table.shape[0], dtype=jnp.int32)[None, :]
    ).astype(jnp.float32)
    factor = jnp.sum(levels * scale_table[None, :], axis=1)
    recon = factor[:, None] * (codes.astype(jnp.float32) - 7.5)
    total_rows = num_rows * lax.axis_size("row")
    cotangent = (
        ((current.reshape(num_rows, width).astype(jnp.float32) - recon) / math.sqrt(total_rows))
        .astype(jnp.bfloat16)
        .reshape(num_rows, local_blocks, BLOCK)
    )
    block_grads = [None] * S
    angle_grads = [None] * S
    for section in reversed(range(S)):
        source, mixed, partner, signs = saved[section]
        upstream = cotangent.astype(jnp.float32)
        angle_grad = jnp.sum(
            upstream
            * (
                -sines[section] * mixed.astype(jnp.float32)
                + signs * cosines[section] * partner.astype(jnp.float32)
            ),
            axis=0,
        )
        outgoing = (signs * sines[section] * upstream).astype(jnp.bfloat16)
        if section < local_bits:
            incoming = swap_halves(outgoing, section)
        else:
            incoming = swapped(outgoing, "dim", section - local_bits)
        direction = (cosines[section] * upstream + incoming.astype(jnp.float32)).astype(
            jnp.bfloat16
        )
        block_grad = jnp.einsum(
            "rnb,rnc->nbc", source, direction, preferred_element_type=jnp.float32
        )
        if section > 0:
            cotangent = jnp.einsum(
                "rnc,nbc->rnb", direction, weights[section], preferred_element_type=jnp.float32
            ).astype(jnp.bfloat16)
        block_grad, angle_grad = lax.psum((block_grad, angle_grad), "row")
        block_grads[section] = block_grad
        angle_grads[section] = angle_grad
    grad_blocks = jnp.stack(block_grads).reshape(S, width, BLOCK)
    grad_angles = jnp.stack(angle_grads).reshape(S, width)
    new_block_state = 0.9 * block_state + 0.1 * grad_blocks * grad_blocks
    step_blocks = grad_blocks / jnp.sqrt(new_block_state)
    new_angle_state = 0.9 * angle_state + 0.1 * grad_angles * grad_angles
    step_angles = grad_angles / jnp.sqrt(new_angle_state)
    return (step_blocks, new_block_state, step_angles, new_angle_state)


def solution(mesh):
    in_specs = (
        P("row", "dim"),
        P(None, "dim", None),
        P(None, "dim"),
        P("row", "dim"),
        P("row"),
        P(),
        P(None, "dim", None),
        P(None, "dim"),
    )
    out_specs = (P(None, "dim", None), P(None, "dim", None), P(None, "dim"), P(None, "dim"))
    return jax.shard_map(local, mesh=mesh, in_specs=in_specs, out_specs=out_specs, check_vma=False)
```

profile of v0, /device:TPU:48, one launch (start us, length us, event | category | flops | bytes accessed | tf_op | source)
XLA Modules:
  0.0 762.4 jit_solution(14621686966139465188)
XLA Ops:
  12.8 2.1 collective-permute-start
  15.4 1.7 collective-permute-done
  17.6 3.2 collective-permute-start.1
  21.4 19.1 %collective-permute-done.1 = bf16[1664,2,128]{2,0,1:T(8,128)(2,1)S(1)} collective-permute-done((bf16[1664,2,128]{2,0,1:T(8,128)(2,1)S(1)}, bf16[1664,2,128]{2,0,1:T(8,128)(2,1)S(1)}, u32[]{:S(2)}, u32[]{:S(2)}) %collective-permute-start.1) | collective-permute-done | bytes 852000 | tf_op jit(solution)/shard_map/ppermute | solution.py:15
  41.1 2.4 collective-permute-start.2
  44.1 20.6 %collective-permute-done.2 = bf16[1664,2,128]{2,0,1:T(8,128)(2,1)S(1)} collective-permute-done((bf16[1664,2,128]{2,0,1:T(8,128)(2,1)S(1)}, bf16[1664,2,128]{2,0,1:T(8,128)(2,1)S(1)}, u32[]{:S(2)}, u32[]{:S(2)}) %collective-permute-start.2) | collective-permute-done | bytes 852000 | tf_op jit(solution)/shard_map/ppermute | solution.py:15
  66.2 14.8 %collective-permute-start.3 = (bf16[1664,2,128]{0,2,1:T(8,128)(2,1)S(1)}, bf16[1664,2,128]{0,2,1:T(8,128)(2,1)S(1)}, u32[]{:S(2)}, u32[]{:S(2)}) collective-permute-start(bf16[1664,2,128]{0,2,1:T(8,128)(2,1)S(1)} %fusion.12), channel_id=1, source_target_pairs={{0,256},{32,288},{64,320},{96,352},{128,384},{160,416},{192,448},{... | collective-permute-start | bytes 2555912 | tf_op jit(solution)/shard_map/ppermute | solution.py:15
  81.7 72.0 %collective-permute-done.3 = bf16[1664,2,128]{0,2,1:T(8,128)(2,1)S(1)} collective-permute-done((bf16[1664,2,128]{0,2,1:T(8,128)(2,1)S(1)}, bf16[1664,2,128]{0,2,1:T(8,128)(2,1)S(1)}, u32[]{:S(2)}, u32[]{:S(2)}) %collective-permute-start.3) | collective-permute-done | bytes 852000 | tf_op jit(solution)/shard_map/ppermute | solution.py:15
  156.1 1.8 copy.43
  157.8 3.0 fusion.38
  160.8 1.8 copy.44
  162.9 12.2 %collective-permute-start.4 = (bf16[1664,2,128]{0,2,1:T(8,128)(2,1)S(1)}, bf16[1664,2,128]{0,2,1:T(8,128)(2,1)S(1)}, u32[]{:S(2)}, u32[]{:S(2)}) collective-permute-start(bf16[1664,2,128]{0,2,1:T(8,128)(2,1)S(1)} %multiply_convert_fusion.4), channel_id=1, source_target_pairs={{0,256},{32,288},{64,320},{96,352},{128,384},{160,416},{192,448},{... | collective-permute-start | bytes 2555912 | tf_op jit(solution)/shard_map/ppermute | solution.py:15
  175.1 61.9 %collective-permute-done.4 = bf16[1664,2,128]{0,2,1:T(8,128)(2,1)S(1)} collective-permute-done((bf16[1664,2,128]{0,2,1:T(8,128)(2,1)S(1)}, bf16[1664,2,128]{0,2,1:T(8,128)(2,1)S(1)}, u32[]{:S(2)}, u32[]{:S(2)}) %collective-permute-start.4) | collective-permute-done | bytes 852000 | tf_op jit(solution)/shard_map/ppermute | solution.py:15
  238.1 2.3 collective-permute-start.5
  240.5 21.3 %collective-permute-done.5 = bf16[1664,2,128]{2,0,1:T(8,128)(2,1)S(1)} collective-permute-done((bf16[1664,2,128]{2,0,1:T(8,128)(2,1)S(1)}, bf16[1664,2,128]{2,0,1:T(8,128)(2,1)S(1)}, u32[]{:S(2)}, u32[]{:S(2)}) %collective-permute-start.5) | collective-permute-done | bytes 852000 | tf_op jit(solution)/shard_map/ppermute | solution.py:15
  263.8 3.2 collective-permute-start.6
  267.0 18.1 %collective-permute-done.6 = bf16[1664,2,128]{2,0,1:T(8,128)(2,1)S(1)} collective-permute-done((bf16[1664,2,128]{2,0,1:T(8,128)(2,1)S(1)}, bf16[1664,2,128]{2,0,1:T(8,128)(2,1)S(1)}, u32[]{:S(2)}, u32[]{:S(2)}) %collective-permute-start.6) | collective-permute-done | bytes 852000 | tf_op jit(solution)/shard_map/ppermute | solution.py:15
  287.1 2.1 collective-permute-start.7
  294.3 2.0 fusion.17
  296.3 2.2 reshape.277
  298.5 2.9 fusion.39
  301.5 1.7 fusion.37
  303.3 105.8 %all-reduce = (f32[1,256]{1,0:T(1,128)S(1)}, f32[1,256]{1,0:T(1,128)S(1)}, f32[1,256]{1,0:T(1,128)S(1)}, f32[1,256]{1,0:T(1,128)S(1)}, f32[1,256]{1,0:T(1,128)S(1)}) all-reduce(f32[1,256]{1,0:T(1,128)S(1)} %bitcast.146, f32[1,256]{1,0:T(1,128)S(1)} %bitcast.145, ...), channel_id=1, replica_groups=mesh['dim'=16,'row'=32] {'row'}, use_global_device_ids=true, to_apply=%region_7.8 | all-reduce | flops 1280 | bytes 10240 | tf_op jit(solution)/shard_map/psum | solution.py:93
  409.7 340.0 %all-reduce.4.cloned.1.call-done = (f32[1,256,128]{2,1,0:T(8,128)}, f32[1,256,128]{2,1,0:T(8,128)}, f32[1,256,128]{2,1,0:T(8,128)}, f32[1,256,128]{2,1,0:T(8,128)}, f32[1,256,128]{2,1,0:T(8,128)}) async-done(((f32[1,256,128]{2,1,0:T(8,128)}, f32[1,256,128]{2,1,0:T(8,128)}, f32[1,256,128]{2,1,0:T(8,128)}, f32[1,256,128]{2,1,0:T(8,128)}, f32[1,256,128]{2,1,0:T(8,128)}), (f32[1,256,128]{2,1,0:T(8,128)}, ...) | async-done | bytes 655376 | tf_op jit(solution)/shard_map/psum | solution.py:93
  (149 shorter events, 29.3 us)
Async XLA Ops:
  7.2 742.6 %all-reduce.4.cloned.1.call-start = ((), (), s32[]{:S(2)}) async-start(), calls=%async_computation | async-start | bytes 1310720 | tf_op jit(solution)/shard_map/psum | solution.py:93
  10.6 29.9 %copy-start.27 = (f32[1,256]{1,0:T(1,128)}, f32[1,256]{1,0:T(1,128)S(1)}, u32[]{:S(2)}) copy-start(f32[1,256]{1,0:T(1,128)S(1)} %get-tuple-element.33) | copy-start | bytes 3076
  12.7 28.3 %copy-start.4 = (bf16[1664,2,128]{2,0,1:T(8,128)(2,1)}, bf16[1664,2,128]{2,0,1:T(8,128)(2,1)S(1)}, u32[]{:S(2)}) copy-start(bf16[1664,2,128]{2,0,1:T(8,128)(2,1)S(1)} %fusion.9) | copy-start | bytes 2555908
  12.8 4.4 collective-permute-start
  17.6 22.9 %collective-permute-start.1 = (bf16[1664,2,128]{2,0,1:T(8,128)(2,1)S(1)}, bf16[1664,2,128]{2,0,1:T(8,128)(2,1)S(1)}, u32[]{:S(2)}, u32[]{:S(2)}) collective-permute-start(bf16[1664,2,128]{2,0,1:T(8,128)(2,1)S(1)} %fusion.10), channel_id=1, source_target_pairs={{0,64},{32,96},{64,0},{96,32},{128,192},{160,224},{192,128},{224,1... | collective-permute-start | bytes 2555912 | tf_op jit(solution)/shard_map/ppermute | solution.py:15
  21.4 44.7 %copy-start.45 = (f32[2,128]{1,0:T(2,128)}, f32[2,128]{1,0:T(2,128)S(1)}, u32[]{:S(2)}) copy-start(f32[2,128]{1,0:T(2,128)S(1)} %get-tuple-element.48) | copy-start | bytes 3076
  41.0 112.7 %copy-start.7 = (bf16[1664,2,128]{2,0,1:T(8,128)(2,1)}, bf16[1664,2,128]{2,0,1:T(8,128)(2,1)S(1)}, u32[]{:S(2)}) copy-start(bf16[1664,2,128]{2,0,1:T(8,128)(2,1)S(1)} %fusion.11) | copy-start | bytes 2555908
  41.0 40.0 %copy-start.35 = (s32[1664]{0:T(1024)S(1)}, s32[1664]{0:T(1024)}, u32[]{:S(2)}) copy-start(s32[1664]{0:T(1024)} %param.12) | copy-start | bytes 19972
  41.1 40.0 %copy-start.51 = (f32[16]{0:T(128)S(1)}, f32[16]{0:T(128)}, u32[]{:S(2)}) copy-start(f32[16]{0:T(128)} %param.13) | copy-start | bytes 196
  41.1 23.7 %collective-permute-start.2 = (bf16[1664,2,128]{2,0,1:T(8,128)(2,1)S(1)}, bf16[1664,2,128]{2,0,1:T(8,128)(2,1)S(1)}, u32[]{:S(2)}, u32[]{:S(2)}) collective-permute-start(bf16[1664,2,128]{2,0,1:T(8,128)(2,1)S(1)} %fusion.11), channel_id=1, source_target_pairs={{0,128},{32,160},{64,192},{96,224},{128,0},{160,32},{192,64},{224,... | collective-permute-start | bytes 2555912 | tf_op jit(solution)/shard_map/ppermute | solution.py:15
  66.2 87.6 %copy-start.2 = (bf16[1664,2,128]{0,2,1:T(8,128)(2,1)}, bf16[1664,2,128]{0,2,1:T(8,128)(2,1)S(1)}, u32[]{:S(2)}) copy-start(bf16[1664,2,128]{0,2,1:T(8,128)(2,1)S(1)} %fusion.12) | copy-start | bytes 2555908
  66.2 87.5 %collective-permute-start.3 = (bf16[1664,2,128]{0,2,1:T(8,128)(2,1)S(1)}, bf16[1664,2,128]{0,2,1:T(8,128)(2,1)S(1)}, u32[]{:S(2)}, u32[]{:S(2)}) collective-permute-start(bf16[1664,2,128]{0,2,1:T(8,128)(2,1)S(1)} %fusion.12), channel_id=1, source_target_pairs={{0,256},{32,288},{64,320},{96,352},{128,384},{160,416},{192,448},{... | collective-permute-start | bytes 2555912 | tf_op jit(solution)/shard_map/ppermute | solution.py:15
  81.7 72.4 %copy-start.31 = (f32[2,128]{1,0:T(2,128)}, f32[2,128]{1,0:T(2,128)S(1)}, u32[]{:S(2)}) copy-start(f32[2,128]{1,0:T(2,128)S(1)} %get-tuple-element.44) | copy-start | bytes 3076
  162.8 74.5 %copy-start.8 = (bf16[1664,2,128]{2,0,1:T(8,128)(2,1)S(1)}, bf16[1664,2,128]{2,0,1:T(8,128)(2,1)}, u32[]{:S(2)}) copy-start(bf16[1664,2,128]{2,0,1:T(8,128)(2,1)} %copy-done.7) | copy-start | bytes 2555908
  162.8 74.5 %copy-start.10 = (bf16[1664,2,128]{2,0,1:T(8,128)(2,1)S(1)}, bf16[1664,2,128]{2,0,1:T(8,128)(2,1)}, u32[]{:S(2)}) copy-start(bf16[1664,2,128]{2,0,1:T(8,128)(2,1)} %copy-done.9) | copy-start | bytes 2555908
  162.8 74.5 %copy-start.30 = (f32[2,128]{1,0:T(2,128)S(1)}, f32[2,128]{1,0:T(2,128)}, u32[]{:S(2)}) copy-start(f32[2,128]{1,0:T(2,128)} %copy-done.29) | copy-start | bytes 3076
  162.8 74.5 %copy-start.49 = (f32[2,128]{1,0:T(2,128)S(1)}, f32[2,128]{1,0:T(2,128)}, u32[]{:S(2)}) copy-start(f32[2,128]{1,0:T(2,128)} %get-tuple-element.45) | copy-start | bytes 3076
  162.8 74.5 %copy-start.50 = (f32[2,128]{1,0:T(2,128)S(1)}, f32[2,128]{1,0:T(2,128)}, u32[]{:S(2)}) copy-start(f32[2,128]{1,0:T(2,128)} %get-tuple-element.56) | copy-start | bytes 3076
  162.9 74.2 %collective-permute-start.4 = (bf16[1664,2,128]{0,2,1:T(8,128)(2,1)S(1)}, bf16[1664,2,128]{0,2,1:T(8,128)(2,1)S(1)}, u32[]{:S(2)}, u32[]{:S(2)}) collective-permute-start(bf16[1664,2,128]{0,2,1:T(8,128)(2,1)S(1)} %multiply_convert_fusion.4), channel_id=1, source_target_pairs={{0,256},{32,288},{64,320},{96,352},{128,384},{160,416},{192,448},{... | collective-permute-start | bytes 2555912 | tf_op jit(solution)/shard_map/ppermute | solution.py:15
  238.1 23.6 %collective-permute-start.5 = (bf16[1664,2,128]{2,0,1:T(8,128)(2,1)S(1)}, bf16[1664,2,128]{2,0,1:T(8,128)(2,1)S(1)}, u32[]{:S(2)}, u32[]{:S(2)}) collective-permute-start(bf16[1664,2,128]{2,0,1:T(8,128)(2,1)S(1)} %get-tuple-element.19), channel_id=1, source_target_pairs={{0,128},{32,160},{64,192},{96,224},{128,0},{160,32},{192,64},{224,... | collective-permute-start | bytes 2555912 | tf_op jit(solution)/shard_map/ppermute | solution.py:15
  263.8 21.3 %collective-permute-start.6 = (bf16[1664,2,128]{2,0,1:T(8,128)(2,1)S(1)}, bf16[1664,2,128]{2,0,1:T(8,128)(2,1)S(1)}, u32[]{:S(2)}, u32[]{:S(2)}) collective-permute-start(bf16[1664,2,128]{2,0,1:T(8,128)(2,1)S(1)} %get-tuple-element.21), channel_id=1, source_target_pairs={{0,64},{32,96},{64,0},{96,32},{128,192},{160,224},{192,128},{224,1... | collective-permute-start | bytes 2555912 | tf_op jit(solution)/shard_map/ppermute | solution.py:15
  287.1 5.8 collective-permute-start.7
  301.5 107.6 %copy-start.36 = (f32[5,256]{1,0:T(8,128)S(1)}, f32[5,256]{1,0:T(8,128)}, u32[]{:S(2)}) copy-start(f32[5,256]{1,0:T(8,128)} %param.15) | copy-start | bytes 15364
  301.5 452.9 %copy-start.18 = (f32[5,256,128]{2,1,0:T(8,128)S(1)}, f32[5,256,128]{2,1,0:T(8,128)}, u32[]{:S(2)}) copy-start(f32[5,256,128]{2,1,0:T(8,128)} %param.14) | copy-start | bytes 1966084
  (37 other events, 225.4 us)
Sparse Core Ops, SparseCore 0:
  301.6 448.1 all-reduce.3
where the time goes:
time: 763 us; the launch traced here: 762 us
  waiting for transfers between devices  555 us (73%)
  blocking collectives  106 us (14%)
  starting transfers between devices  42.4 us (6%)
  local copies, waits for them, and re-layouts  16.7 us (2%)
  between operations  14.7 us (2%)
  other arithmetic  14.1 us (2%)
  matrix products  13.9 us (2%)
    psum x1, waiting for transfers between devices, local(): block_grad, angle_grad = lax.psum((block_grad, angle_grad), 'row')  340 us
    ppermute x8, waiting for transfers between devices, swapped(): return lax.ppermute(value, axis, pairs)  215 us
    psum x1, blocking collectives, local(): block_grad, angle_grad = lax.psum((block_grad, angle_grad), 'row')  106 us
    ppermute x8, starting transfers between devices, swapped(): return lax.ppermute(value, axis, pairs)  42.3 us
  transfers between devices with their start and end apart: 9, of which 8 were waited for; matrix products, arithmetic and copies ran while one was open for 1% of the time, Pallas kernels for 0%

commit v1 on v0

v1 whole, which is shorter than its diff:
```python
import math

import jax
import jax.numpy as jnp
from jax import lax
from jax.experimental import pallas as pl
from jax.experimental.pallas import tpu as pltpu
from jax.sharding import PartitionSpec as P

BLOCK = 128
S = 5
W = 256
R = 208
SUB = 16
XS = S * W // 4
ZS = XS // 4
MESH = pl.DeviceIdType.MESH
F32 = jnp.float32
BF16 = jnp.bfloat16


def flip(value, mask):
    for bit in (1, 2, 4, 8):
        if mask & bit:
            value = value + bit * (1 - 2 * ((value // bit) % 2))
    return value


def swap(value):
    return jnp.concatenate([value[:, BLOCK:], value[:, :BLOCK]], axis=1)


def fold(value):
    return jnp.sum(value.reshape(-1, 8, value.shape[-1]), axis=0)


def make_kernel(home_rows, total_rows):
    n = home_rows // R
    scale = 1.0 / math.sqrt(total_rows)

    def kernel(
        vec, codes, w, ang, idx, tab, grad_o, ang_o,
        u, v, vp, gs, qs, qp, dv, cod, codsend, wb, trig, fc, fac, acc, sa, sb,
        sx, rx, sxs, sz, rz, szs, sk, rk, gx,
        lsem, w_s, w_r, t_s, t_r, v_s, v_r, c_s, c_r, f_s, f_r, b_s, b_r, r_s, r_r,
    ):
        d = lax.axis_index("dim")
        r = lax.axis_index("row")
        zh, y, c = d // 8, (d // 2) % 4, d % 2
        x, zl = r // 8, r % 8
        kk, ii = zh * 2 + zl // 4, zl % 4

        def device(zh=zh, y=y, c=c, x=x, kk=None, ii=ii):
            lo = zl // 4
            if kk is not None:
                zh, lo = kk // 2, kk % 2
            return (zh * 8 + y * 2 + c, x * 8 + lo * 4 + ii)

        across = device(zh=1 - zh)
        core = device(c=1 - c)
        y_near, y_far = device(y=flip(y, 1)), device(y=flip(y, 2))
        x_peers = [device(x=flip(x, m)) for m in (1, 2, 3)]
        i_peers = [device(ii=flip(ii, m)) for m in (1, 2, 3)]
        k_peers = [device(kk=flip(kk, m)) for m in (1, 2, 3)]
        partners = [None, core, y_near, y_far]
        greeted = [core, y_near, y_far] + x_peers + i_peers + k_peers

        def remote(src, dst, send, recv, target):
            return pltpu.make_async_remote_copy(
                src_ref=src, dst_ref=dst, send_sem=send, recv_sem=recv,
                device_id=target, device_id_type=MESH,
            )

        barrier = pltpu.get_barrier_semaphore()
        for target in greeted:
            pl.semaphore_signal(barrier, inc=1, device_id=target, device_id_type=MESH)

        wb[0] = w[...].astype(BF16)
        lane = lax.broadcasted_iota(jnp.int32, (1, W), 1)
        bits = [jnp.where(lane < BLOCK, 1.0, -1.0).astype(F32)]
        for bit in (c, y % 2, y // 2, zh):
            bits.append(jnp.full((1, W), (1 - 2 * bit).astype(F32), F32))
        trig[0, 0:S] = jnp.cos(ang[...])
        sines = jnp.sin(ang[...])
        for s in range(S):
            trig[0, 8 + s : 9 + s] = bits[s] * sines[s : s + 1]
        acc[...] = jnp.zeros_like(acc)
        sa[...] = jnp.zeros_like(sa)
        sb[...] = jnp.zeros_like(sb)
        pl.semaphore_wait(barrier, len(greeted))

        home = pl.multiple_of(zh * home_rows, 64)
        away = pl.multiple_of((1 - zh) * home_rows, 64)

        def weight_copy(step):
            rows = pl.ds(pl.multiple_of(x * XS, 64), XS)
            if step == 0:
                return remote(wb.at[0, rows], wb.at[1, rows], w_s.at[0], w_r.at[0], across)
            return remote(
                wb.at[1, rows], wb.at[1, rows], w_s.at[step], w_r.at[step], x_peers[step - 1]
            )

        def trig_copy():
            return remote(trig.at[0], trig.at[1], t_s.at[0], t_r.at[0], across)

        def vec_copy(j):
            rows = pl.ds(pl.multiple_of(away + j * R, 16), R)
            return remote(vec.at[rows], u.at[0, n + j], v_s.at[j], v_r.at[j], across)

        def own_copy(j):
            rows = pl.ds(pl.multiple_of(home + j * R, 16), R)
            return pltpu.make_async_copy(vec.at[rows], u.at[0, j], lsem.at[j])

        def code_copy(j):
            return remote(codsend.at[j], cod.at[j], c_s.at[j], c_r.at[j], across)

        def fwd_copy(s, i):
            return remote(
                v.at[s, i], vp.at[s - 1, i], f_s.at[s - 1, i], f_r.at[s - 1, i], partners[s]
            )

        def bwd_copy(s, j):
            return remote(
                qs.at[s - 1, j], qp.at[s - 1, j], b_s.at[s - 1, j], b_r.at[s - 1, j], partners[s]
            )

        weight_copy(0).start()
        trig_copy().start()
        for j in range(n):
            own_copy(j).start()
        for j in range(n):
            vec_copy(j).start()

        def rows_of(k):
            return pl.ds(pl.multiple_of(k * SUB, SUB), SUB)

        for j in range(n):

            def convert(k, carry, j=j):
                rows = pl.ds(pl.multiple_of(away + j * R + k * SUB, 16), SUB)
                codsend[j, rows_of(k)] = codes[rows].astype(F32).astype(BF16)
                return carry

            lax.fori_loop(0, R // SUB, convert, 0)
            code_copy(j).start()
        index = idx[...]
        factor = jnp.zeros(index.shape, F32)
        for level in range(tab.shape[0]):
            factor = jnp.where(index == level, tab[level], factor)
        fc[0 : index.shape[0]] = factor

        def spread(p, carry):
            piece = zh * (home_rows // 64) + p
            row = fc[pl.ds(piece // 2, 1)]
            at = lax.broadcasted_iota(jnp.int32, (64, BLOCK), 1)
            want = lax.broadcasted_iota(jnp.int32, (64, BLOCK), 0) + 64 * (piece % 2)
            column = jnp.sum(jnp.where(at == want, row, 0.0), axis=1, keepdims=True)
            fac[pl.ds(pl.multiple_of(p * 64, 64), 64)] = jnp.broadcast_to(column, (64, BLOCK))
            return carry

        lax.fori_loop(0, home_rows // 64, spread, 0)

        def wrow(s, b):
            return pl.ds(s * W + b * BLOCK, BLOCK)

        def lanes(b):
            return pl.ds(b * BLOCK, BLOCK)

        def cos_of(h, s):
            return trig[h, pl.ds(s, 1)]

        def sin_of(h, s):
            return trig[h, pl.ds(8 + s, 1)]

        def mix(s, i, h):
            for b in range(2):
                v[s, i, :, lanes(b)] = jnp.dot(
                    u[s, i, :, lanes(b)], wb[h, wrow(s, b)], preferred_element_type=F32
                ).astype(BF16)

        def combine(s, i, h):
            cosine, sine = cos_of(h, s), sin_of(h, s)

            def step(k, carry):
                rows = rows_of(k)
                mine = v[s, i, rows].astype(F32)
                theirs = swap(mine) if s == 0 else vp[s - 1, i, rows].astype(F32)
                u[s + 1, i, rows] = (cosine * mine + sine * theirs).astype(BF16)
                return carry

            lax.fori_loop(0, R // SUB, step, 0)

        def forward(t, carry):
            for s in (3, 2, 1):
                i = t - s

                @pl.when((i >= 0) & (i < 2 * n))
                def _(s=s, i=i):
                    h = i // n
                    fwd_copy(s, i).wait_recv()
                    combine(s, i, h)
                    mix(s + 1, i, h)
                    if s < 3:
                        fwd_copy(s + 1, i).start()

            @pl.when(t == 2)
            def _():
                weight_copy(0).wait_recv()
                for step in (1, 2, 3):
                    weight_copy(step).start()

            @pl.when(t == n)
            def _():
                for step in (1, 2, 3):
                    weight_copy(step).wait_recv()
                trig_copy().wait_recv()

            @pl.when(t < n)
            def _():
                own_copy(t).wait()

            @pl.when((t >= n) & (t < 2 * n))
            def _():
                vec_copy(t - n).wait_recv()

            @pl.when(t < 2 * n)
            def _():
                h = t // n
                mix(0, t, h)
                combine(0, t, h)
                mix(1, t, h)
                fwd_copy(1, t).start()

            return carry

        lax.fori_loop(0, 2 * n + 3, forward, 0)

        def weight_grad(s, j):
            for h in range(2):
                for b in range(2):
                    acc[h, wrow(s, b)] += lax.dot_general(
                        u[s, h * n + j, :, lanes(b)],
                        dv[h, :, lanes(b)],
                        (((0,), (0,)), ((), ())),
                        preferred_element_type=F32,
                    )

        def pull(s, j):
            t = s - 1
            for h in range(2):
                i = h * n + j
                slot = max(t, 1) - 1
                for b in range(2):
                    gs[slot, j, h, :, lanes(b)] = lax.dot_general(
                        dv[h, :, lanes(b)],
                        wb[h, wrow(s, b)],
                        (((1,), (1,)), ((), ())),
                        preferred_element_type=F32,
                    ).astype(BF16)
            for h in range(2):
                i = h * n + j
                cosine, sine = cos_of(h, t), sin_of(h, t)

                def step(k, sums, h=h, i=i, cosine=cosine, sine=sine):
                    rows = rows_of(k)
                    up = gs[slot, j, h, rows].astype(F32)
                    mine = v[t, i, rows].astype(F32)
                    theirs = swap(mine) if t == 0 else vp[t - 1, i, rows].astype(F32)
                    sent = (sine * up).astype(BF16)
                    if t == 0:
                        dv[h, rows] = (cosine * up + swap(sent.astype(F32))).astype(BF16)
                    else:
                        qs[t - 1, j, h, rows] = sent
                    return sums[0] + fold(up * mine), sums[1] + fold(up * theirs)

                one, two = lax.fori_loop(0, R // SUB, step, (sa[h, t], sb[h, t]))
                sa[h, t] = one
                sb[h, t] = two

        def turn(j):
            code_copy(j).wait_recv()
            cos_a, sin_a, cos_b, sin_b = cos_of(0, 4), sin_of(0, 4), cos_of(1, 4), sin_of(1, 4)

            def step(k, sums):
                rows = rows_of(k)
                va, vb = v[4, j, rows].astype(F32), v[4, n + j, rows].astype(F32)
                f = fac[pl.ds(pl.multiple_of(j * R + k * SUB, 16), SUB)]
                f = jnp.concatenate([f, f], axis=1)
                own = codes[pl.ds(pl.multiple_of(home + j * R + k * SUB, 16), SUB)].astype(F32)
                recon_a = f * (own - 7.5)
                recon_b = f * (cod[j, rows].astype(F32) - 7.5)
                ua = (cos_a * va + sin_a * vb).astype(BF16).astype(F32)
                ub = (cos_b * vb + sin_b * va).astype(BF16).astype(F32)
                ga = ((ua - recon_a) * scale).astype(BF16).astype(F32)
                gb = ((ub - recon_b) * scale).astype(BF16).astype(F32)
                qa = (sin_a * ga).astype(BF16).astype(F32)
                qb = (sin_b * gb).astype(BF16).astype(F32)
                dv[0, rows] = (cos_a * ga + qb).astype(BF16)
                dv[1, rows] = (cos_b * gb + qa).astype(BF16)
                return (
                    sums[0] + fold(ga * va),
                    sums[1] + fold(ga * vb),
                    sums[2] + fold(gb * vb),
                    sums[3] + fold(gb * va),
                )

            sums = lax.fori_loop(0, R // SUB, step, (sa[0, 4], sb[0, 4], sa[1, 4], sb[1, 4]))
            sa[0, 4], sb[0, 4], sa[1, 4], sb[1, 4] = sums
            weight_grad(4, j)
            pull(4, j)
            bwd_copy(3, j).start()

        def back(s, j):
            bwd_copy(s, j).wait_recv()
            for h in range(2):
                cosine = cos_of(h, s)

                def step(k, carry, h=h, cosine=cosine):
                    rows = rows_of(k)
                    up = gs[s - 1, j, h, rows].astype(F32)
                    dv[h, rows] = (cosine * up + qp[s - 1, j, h, rows].astype(F32)).astype(BF16)
                    return carry

                lax.fori_loop(0, R // SUB, step, 0)
            weight_grad(s, j)
            pull(s, j)
            if s > 1:
                bwd_copy(s - 1, j).start()
            else:
                weight_grad(0, j)

        def backward(t, carry):
            for s in (1, 2, 3):
                j = t - (4 - s)

                @pl.when((j >= 0) & (j < n))
                def _(s=s, j=j):
                    back(s, j)

            @pl.when(t < n)
            def _():
                turn(t)

            return carry

        lax.fori_loop(0, n + 3, backward, 0)

        turned = []
        for h in range(2):
            parts = []
            for s in range(S):
                a = jnp.sum(sa[h, s], axis=0, keepdims=True)
                b = jnp.sum(sb[h, s], axis=0, keepdims=True)
                sign = bits[s] if (h == 0 or s < 4) else -bits[s]
                whole = sign * (cos_of(h, s) * b - sin_of(h, s) * a)
                parts += [whole[:, :BLOCK], whole[:, BLOCK:]]
            parts.append(jnp.zeros((6, BLOCK), F32))
            turned.append(jnp.concatenate(parts, axis=0).astype(BF16))
        angles = jnp.concatenate(turned, axis=0)

        def fill_x(ref, p):
            for h in range(2):
                ref[pl.ds(h * XS, XS)] = acc[h, pl.ds(pl.multiple_of(p * XS, 64), XS)].astype(BF16)
            ref[pl.ds(2 * XS, 32)] = angles

        def x_copy(m):
            return remote(sx.at[m], rx.at[x], r_s.at[m], r_r.at[m], x_peers[m])

        def i_copy(m):
            return remote(sz.at[m], rz.at[ii], r_s.at[3 + m], r_r.at[3 + m], i_peers[m])

        def k_copy(m):
            return remote(sk.at[m], rk.at[kk], r_s.at[6 + m], r_r.at[6 + m], k_peers[m])

        def gi_copy(m):
            rows = pl.ds(pl.multiple_of(ii * ZS, 16), ZS)
            return remote(
                gx.at[x, rows], gx.at[x, rows], r_s.at[9 + m], r_r.at[9 + m], i_peers[m]
            )

        def gx_copy(m):
            return remote(gx.at[x], gx.at[x], r_s.at[12 + m], r_r.at[12 + m], x_peers[m])

        for m in range(3):
            fill_x(sx.at[m], flip(x, m + 1))
            x_copy(m).start()
        fill_x(rx.at[x], x)
        for m in range(3):
            x_copy(m).wait_recv()
        sxs[...] = (rx[0].astype(F32) + rx[1].astype(F32)) + (rx[2].astype(F32) + rx[3].astype(F32))

        def fill_z(ref, p):
            for h in range(2):
                ref[pl.ds(h * ZS, ZS)] = sxs[
                    pl.ds(pl.multiple_of(h * XS + p * ZS, 16), ZS)
                ].astype(BF16)
            ref[pl.ds(2 * ZS, 32)] = sxs[pl.ds(2 * XS, 32)].astype(BF16)

        for m in range(3):
            fill_z(sz.at[m], flip(ii, m + 1))
            i_copy(m).start()
        fill_z(rz.at[ii], ii)
        for m in range(3):
            i_copy(m).wait_recv()
        szs[...] = (rz[0].astype(F32) + rz[1].astype(F32)) + (rz[2].astype(F32) + rz[3].astype(F32))

        def fill_k(ref, h):
            ref[pl.ds(0, ZS)] = szs[pl.ds(h * ZS, ZS)].astype(BF16)
            ref[pl.ds(ZS, 16)] = szs[pl.ds(2 * ZS + h * 16, 16)].astype(BF16)

        for m in range(3):
            fill_k(sk.at[m], 0 if m == 0 else 1)
            k_copy(m).start()
        fill_k(rk.at[kk], 0)
        for m in range(3):
            k_copy(m).wait_recv()
        final = (rk[0].astype(F32) + rk[1].astype(F32)) + (rk[2].astype(F32) + rk[3].astype(F32))
        ang_o[...] = final[ZS:]
        gx[x, pl.ds(pl.multiple_of(ii * ZS, 16), ZS)] = final[:ZS].astype(BF16)

        for m in range(3):
            gi_copy(m).start()
        for m in range(3):
            gi_copy(m).wait_recv()
        for m in range(3):
            gx_copy(m).start()
        for m in range(3):
            gx_copy(m).wait_recv()
        for p in range(4):
            grad_o[pl.ds(p * XS, XS)] = gx[p].astype(F32)

        for step in range(4):
            weight_copy(step).wait_send()
        trig_copy().wait_send()

        def drain(j, carry):
            vec_copy(j).wait_send()
            code_copy(j).wait_send()
            for s in (1, 2, 3):
                fwd_copy(s, j).wait_send()
                fwd_copy(s, n + j).wait_send()
                bwd_copy(s, j).wait_send()
            return carry

        lax.fori_loop(0, n, drain, 0)
        for m in range(3):
            for copy in (x_copy, i_copy, k_copy, gi_copy, gx_copy):
                copy(m).wait_send()

    return kernel, n


def gradients(vectors, blocks, angles, codes, scale_index, scale_table):
    num_rows = vectors.shape[0]
    kernel, n = make_kernel(num_rows // 2, num_rows * 32)
    vmem = pl.BlockSpec(memory_space=pltpu.VMEM)
    dma = pltpu.SemaphoreType.DMA
    shapes = [
        pltpu.VMEM((S, 2 * n, R, W), BF16),
        pltpu.VMEM((S, 2 * n, R, W), BF16),
        pltpu.VMEM((3, 2 * n, R, W), BF16),
        pltpu.VMEM((3, n, 2, R, W), BF16),
        pltpu.VMEM((3, n, 2, R, W), BF16),
        pltpu.VMEM((3, n, 2, R, W), BF16),
        pltpu.VMEM((2, R, W), BF16),
        pltpu.VMEM((n, R, W), BF16),
        pltpu.VMEM((n, R, W), BF16),
        pltpu.VMEM((2, S * W, BLOCK), BF16),
        pltpu.VMEM((2, 16, W), F32),
        pltpu.VMEM((16, BLOCK), F32),
        pltpu.VMEM((num_rows // 2, BLOCK), F32),
        pltpu.VMEM((2, S * W, BLOCK), F32),
        pltpu.VMEM((2, S, 8, W), F32),
        pltpu.VMEM((2, S, 8, W), F32),
        pltpu.VMEM((3, 2 * XS + 32, BLOCK), BF16),
        pltpu.VMEM((4, 2 * XS + 32, BLOCK), BF16),
        pltpu.VMEM((2 * XS + 32, BLOCK), F32),
        pltpu.VMEM((3, 2 * ZS + 32, BLOCK), BF16),
        pltpu.VMEM((4, 2 * ZS + 32, BLOCK), BF16),
        pltpu.VMEM((2 * ZS + 32, BLOCK), F32),
        pltpu.VMEM((3, ZS + 16, BLOCK), BF16),
        pltpu.VMEM((4, ZS + 16, BLOCK), BF16),
        pltpu.VMEM((4, XS, BLOCK), BF16),
        dma((n,)),
        dma((4,)), dma((4,)), dma((1,)), dma((1,)), dma((n,)), dma((n,)), dma((n,)), dma((n,)),
        dma((3, 2 * n)), dma((3, 2 * n)), dma((3, n)), dma((3, n)), dma((15,)), dma((15,)),
    ]
    return pl.pallas_call(
        kernel,
        name="butterfly",
        out_shape=(
            jax.ShapeDtypeStruct((S * W, BLOCK), F32),
            jax.ShapeDtypeStruct((16, BLOCK), F32),
        ),
        in_specs=[
            pl.BlockSpec(memory_space=pl.ANY),
            vmem, vmem, vmem, vmem,
            pl.BlockSpec(memory_space=pltpu.SMEM),
        ],
        out_specs=(vmem, vmem),
        scratch_shapes=shapes,
        compiler_params=pltpu.CompilerParams(
            collective_id=0, has_side_effects=True, vmem_limit_bytes=56 * 2**20
        ),
    )(
        vectors, codes, blocks.reshape(S * W, BLOCK), angles,
        scale_index.reshape(num_rows // BLOCK, BLOCK), scale_table,
    )


def local(vectors, blocks, angles, codes, scale_index, scale_table, block_state, angle_state):
    grad, turned = gradients(vectors, blocks, angles, codes, scale_index, scale_table)
    grad_blocks = grad.reshape(S, W, BLOCK)
    grad_angles = turned[: 2 * S].reshape(S, W)
    new_block_state = 0.9 * block_state + 0.1 * grad_blocks * grad_blocks
    step_blocks = grad_blocks / jnp.sqrt(new_block_state)
    new_angle_state = 0.9 * angle_state + 0.1 * grad_angles * grad_angles
    step_angles = grad_angles / jnp.sqrt(new_angle_state)
    return (step_blocks, new_block_state, step_angles, new_angle_state)


def solution(mesh):
    in_specs = (
        P("row", "dim"),
        P(None, "dim", None),
        P(None, "dim"),
        P("row", "dim"),
        P("row"),
        P(),
        P(None, "dim", None),
        P(None, "dim"),
    )
    out_specs = (P(None, "dim", None), P(None, "dim", None), P(None, "dim"), P(None, "dim"))
    return jax.shard_map(local, mesh=mesh, in_specs=in_specs, out_specs=out_specs, check_vma=False)
```

time: 763 us -> 200 us (0.26)
  the two profiles are of different devices: /device:TPU:48 before, /device:TPU:1 now
where the time goes in v1:
time: 200 us; the launch traced here: 199 us
  Pallas kernels  196 us (98%)
  other arithmetic  2.89 us (1%)
    pallas_call x1, Pallas kernels, gradients(): pl.pallas_call(kernel, name='butterfly', out_shape=(jax.ShapeDtypeStruct(...  196 us

profile of v1, /device:TPU:1, one launch (start us, length us, event | category | flops | bytes accessed | tf_op | source)
XLA Modules:
  0.0 199.5 jit_solution(10160282942895169751)
XLA Ops:
  0.6 0.0 copy-start
  0.6 195.9 %butterfly.1 = (f32[1280,128]{1,0:T(8,128)}, f32[16,128]{1,0:T(8,128)}) custom-call(bf16[1664,256]{1,0:T(8,128)(2,1)} %vec.1, s32[1664,256]{1,0:T(8,128)} %codes.1, f32[1280,128]{1,0:T(8,128)} %bitcast.5, f32[5,256]{1,0:T(8,128)} %ang.1, s32[13,128]{1,0:T(8,128)} %bitcast.6, f32[16]{0:T(128)} %tab.1), custom_call_target="tpu_custom_call" | custom-call | tf_op jit(solution)/shard_map/butterfly/pallas_call | solution.py:488
  196.5 0.0 copy-start.1
  196.5 0.0 copy-start.2
  196.5 0.0 copy-done
  196.6 2.3 %rsqrt_multiply_fusion = (f32[5,256,128]{2,1,0:T(8,128)}, f32[5,256,128]{2,1,0:T(8,128)}) fusion(f32[5,256,128]{2,1,0:T(8,128)} %bitcast.4, f32[5,256,128]{2,1,0:T(8,128)S(1)} %copy-done), kind=kLoop, calls=%fused_computation.2 | loop fusion | flops 819200 | bytes 2621440 | tf_op jit(solution)/shard_map/div | solution.py:516
  198.8 0.0 copy-done.1
  198.8 0.0 copy-done.2
  198.8 0.6 rsqrt_multiply_fusion.1
  (1 shorter events, 0.0 us)
Async XLA Ops:
  0.6 195.9 %copy-start = (f32[5,256,128]{2,1,0:T(8,128)S(1)}, f32[5,256,128]{2,1,0:T(8,128)}, u32[]{:S(2)}) copy-start(f32[5,256,128]{2,1,0:T(8,128)} %param.14) | copy-start | bytes 1966084
  196.5 2.3 %copy-start.1 = (f32[16,128]{1,0:T(8,128)S(1)}, f32[16,128]{1,0:T(8,128)}, u32[]{:S(2)}) copy-start(f32[16,128]{1,0:T(8,128)} %get-tuple-element.7) | copy-start | bytes 24580
  196.5 2.3 %copy-start.2 = (f32[5,256]{1,0:T(8,128)S(1)}, f32[5,256]{1,0:T(8,128)}, u32[]{:S(2)}) copy-start(f32[5,256]{1,0:T(8,128)} %param.15) | copy-start | bytes 15364

commit v2 on v1

--- a/solution.py
+++ b/solution.py
@@ -10,10 +10,15 @@
 BLOCK = 128
 S = 5
 W = 256
-R = 208
+R = 64
 SUB = 16
 XS = S * W // 4
 ZS = XS // 4
+XP = W // 4
+ZP = XP // 4
+AHEAD = 6
+WINDOW = 4
+LAG = 9
 MESH = pl.DeviceIdType.MESH
 F32 = jnp.float32
 BF16 = jnp.bfloat16
@@ -40,7 +45,7 @@
 
     def kernel(
         vec, codes, w, ang, idx, tab, grad_o, ang_o,
-        u, v, vp, gs, qs, qp, dv, cod, codsend, wb, trig, fc, fac, acc, sa, sb,
+        u, v, vp, gs, qs, qp, dv, cod, codsend, wb, trig, ang2, fc, fac, acc, sa, sb,
         sx, rx, sxs, sz, rz, szs, sk, rk, gx,
         lsem, w_s, w_r, t_s, t_r, v_s, v_r, c_s, c_r, f_s, f_r, b_s, b_r, r_s, r_r,
     ):
@@ -76,73 +81,87 @@
             pl.semaphore_signal(barrier, inc=1, device_id=target, device_id_type=MESH)
 
         wb[0] = w[...].astype(BF16)
+        pl.semaphore_wait(barrier, len(greeted))
+
+        home = pl.multiple_of(zh * home_rows, 64)
+        away = pl.multiple_of((1 - zh) * home_rows, 64)
+
+        def weight_copy(step):
+            whole = pl.ds(pl.multiple_of(x * XS, 64), XS)
+            piece = pl.ds(pl.multiple_of(x * XS + ii * ZS, 16), ZS)
+            if step == 0:
+                source, rows, target = 0, piece, across
+            elif step < 4:
+                source, rows, target = 1, piece, i_peers[step - 1]
+            else:
+                source, rows, target = 1, whole, x_peers[step - 4]
+            return remote(wb.at[source, rows], wb.at[1, rows], w_s.at[step], w_r.at[step], target)
+
+        def angle_copy():
+            return remote(ang, ang2, t_s.at[0], t_r.at[0], across)
+
+        def vec_copy(j):
+            rows = pl.ds(pl.multiple_of(away + j * R, 16), R)
+            return remote(vec.at[rows], u.at[0, n + j], v_s.at[j], v_r.at[j], across)
+
+        def own_copy(j):
+            rows = pl.ds(pl.multiple_of(home + j * R, 16), R)
+            return pltpu.make_async_copy(vec.at[rows], u.at[0, j], lsem.at[j])
+
+        def code_copy(j):
+            return remote(codsend.at[j], cod.at[j], c_s.at[j], c_r.at[j], across)
+
+        def fwd_copy(s, i):
+            return remote(
+                v.at[s, i], vp.at[s - 1, i], f_s.at[s - 1, i], f_r.at[s - 1, i], partners[s]
+            )
+
+        def bwd_copy(s, j):
+            return remote(
+                qs.at[s - 1, j], qp.at[s - 1, j], b_s.at[s - 1, j], b_r.at[s - 1, j], partners[s]
+            )
+
+        vec_copy(0).start()
+        weight_copy(0).start()
+        angle_copy().start()
+        for j in range(n):
+            own_copy(j).start()
+
+        def steps(step, carry=None):
+            for k in range(R // SUB):
+                carry = step(k, carry)
+            return carry
+
+        def rows_of(k):
+            return pl.ds(k * SUB, SUB)
+
+        def send_codes(j):
+            def step(k, carry):
+                rows = pl.ds(pl.multiple_of(away + j * R + k * SUB, 16), SUB)
+                codsend[j, rows_of(k)] = codes[rows].astype(F32).astype(BF16)
+
+            steps(step)
+            code_copy(j).start()
+
+        for j in range(1, WINDOW):
+            vec_copy(j).start()
+
         lane = lax.broadcasted_iota(jnp.int32, (1, W), 1)
         bits = [jnp.where(lane < BLOCK, 1.0, -1.0).astype(F32)]
         for bit in (c, y % 2, y // 2, zh):
             bits.append(jnp.full((1, W), (1 - 2 * bit).astype(F32), F32))
-        trig[0, 0:S] = jnp.cos(ang[...])
-        sines = jnp.sin(ang[...])
-        for s in range(S):
-            trig[0, 8 + s : 9 + s] = bits[s] * sines[s : s + 1]
+
+        def twiddle(h, theta):
+            trig[h, 0:S] = jnp.cos(theta)
+            sines = jnp.sin(theta)
+            for s in range(S):
+                sign = bits[s] if (h == 0 or s < 4) else -bits[s]
+                trig[h, 8 + s : 9 + s] = sign * sines[s : s + 1]
+
+        twiddle(0, ang[...])
         acc[...] = jnp.zeros_like(acc)
         sa[...] = jnp.zeros_like(sa)
         sb[...] = jnp.zeros_like(sb)
-        pl.semaphore_wait(barrier, len(greeted))
-
-        home = pl.multiple_of(zh * home_rows, 64)
-        away = pl.multiple_of((1 - zh) * home_rows, 64)
-
-        def weight_copy(step):
-            rows = pl.ds(pl.multiple_of(x * XS, 64), XS)
-            if step == 0:
-                return remote(wb.at[0, rows], wb.at[1, rows], w_s.at[0], w_r.at[0], across)
-            return remote(
-                wb.at[1, rows], wb.at[1, rows], w_s.at[step], w_r.at[step], x_peers[step - 1]
-            )
-
-        def trig_copy():
-            return remote(trig.at[0], trig.at[1], t_s.at[0], t_r.at[0], across)
-
-        def vec_copy(j):
-            rows = pl.ds(pl.multiple_of(away + j * R, 16), R)
-            return remote(vec.at[rows], u.at[0, n + j], v_s.at[j], v_r.at[j], across)
-
-        def own_copy(j):
-            rows = pl.ds(pl.multiple_of(home + j * R, 16), R)
-            return pltpu.make_async_copy(vec.at[rows], u.at[0, j], lsem.at[j])
-
-        def code_copy(j):
-            return remote(codsend.at[j], cod.at[j], c_s.at[j], c_r.at[j], across)
-
-        def fwd_copy(s, i):
-            return remote(
-                v.at[s, i], vp.at[s - 1, i], f_s.at[s - 1, i], f_r.at[s - 1, i], partners[s]
-            )
-
-        def bwd_copy(s, j):
-            return remote(
-                qs.at[s - 1, j], qp.at[s - 1, j], b_s.at[s - 1, j], b_r.at[s - 1, j], partners[s]
-            )
-
-        weight_copy(0).start()
-        trig_copy().start()
-        for j in range(n):
-            own_copy(j).start()
-        for j in range(n):
-            vec_copy(j).start()
-
-        def rows_of(k):
-            return pl.ds(pl.multiple_of(k * SUB, SUB), SUB)
-
-        for j in range(n):
-
-            def convert(k, carry, j=j):
-                rows = pl.ds(pl.multiple_of(away + j * R + k * SUB, 16), SUB)
-                codsend[j, rows_of(k)] = codes[rows].astype(F32).astype(BF16)
-                return carry
-
-            lax.fori_loop(0, R // SUB, convert, 0)
-            code_copy(j).start()
         index = idx[...]
         factor = jnp.zeros(index.shape, F32)
         for level in range(tab.shape[0]):
@@ -186,54 +205,21 @@
                 mine = v[s, i, rows].astype(F32)
                 theirs = swap(mine) if s == 0 else vp[s - 1, i, rows].astype(F32)
                 u[s + 1, i, rows] = (cosine * mine + sine * theirs).astype(BF16)
-                return carry
-
-            lax.fori_loop(0, R // SUB, step, 0)
-
-        def forward(t, carry):
-            for s in (3, 2, 1):
-                i = t - s
-
-                @pl.when((i >= 0) & (i < 2 * n))
-                def _(s=s, i=i):
-                    h = i // n
-                    fwd_copy(s, i).wait_recv()
-                    combine(s, i, h)
-                    mix(s + 1, i, h)
-                    if s < 3:
-                        fwd_copy(s + 1, i).start()
-
-            @pl.when(t == 2)
-            def _():
-                weight_copy(0).wait_recv()
-                for step in (1, 2, 3):
-                    weight_copy(step).start()
-
-            @pl.when(t == n)
-            def _():
-                for step in (1, 2, 3):
-                    weight_copy(step).wait_recv()
-                trig_copy().wait_recv()
-
-            @pl.when(t < n)
-            def _():
-                own_copy(t).wait()
-
-            @pl.when((t >= n) & (t < 2 * n))
-            def _():
-                vec_copy(t - n).wait_recv()
-
-            @pl.when(t < 2 * n)
-            def _():
-                h = t // n
-                mix(0, t, h)
-                combine(0, t, h)
-                mix(1, t, h)
-                fwd_copy(1, t).start()
-
-            return carry
-
-        lax.fori_loop(0, 2 * n + 3, forward, 0)
+
+            steps(step)
+
+        def start(i, h):
+            mix(0, i, h)
+            combine(0, i, h)
+            mix(1, i, h)
+            fwd_copy(1, i).start()
+
+        def carry_on(s, i, h):
+            fwd_copy(s, i).wait_recv()
+            combine(s, i, h)
+            mix(s + 1, i, h)
+            if s < 3:
+                fwd_copy(s + 1, i).start()
 
         def weight_grad(s, j):
             for h in range(2):
@@ -273,7 +259,7 @@
                         qs[t - 1, j, h, rows] = sent
                     return sums[0] + fold(up * mine), sums[1] + fold(up * theirs)
 
-                one, two = lax.fori_loop(0, R // SUB, step, (sa[h, t], sb[h, t]))
+                one, two = steps(step, (sa[h, t], sb[h, t]))
                 sa[h, t] = one
                 sb[h, t] = two
 
@@ -304,7 +290,7 @@
                     sums[3] + fold(gb * va),
                 )
 
-            sums = lax.fori_loop(0, R // SUB, step, (sa[0, 4], sb[0, 4], sa[1, 4], sb[1, 4]))
+            sums = steps(step, (sa[0, 4], sb[0, 4], sa[1, 4], sb[1, 4]))
             sa[0, 4], sb[0, 4], sa[1, 4], sb[1, 4] = sums
             weight_grad(4, j)
             pull(4, j)
@@ -319,9 +305,8 @@
                     rows = rows_of(k)
                     up = gs[s - 1, j, h, rows].astype(F32)
                     dv[h, rows] = (cosine * up + qp[s - 1, j, h, rows].astype(F32)).astype(BF16)
-                    return carry
-
-                lax.fori_loop(0, R // SUB, step, 0)
+
+                steps(step)
             weight_grad(s, j)
             pull(s, j)
             if s > 1:
@@ -329,21 +314,92 @@
             else:
                 weight_grad(0, j)
 
-        def backward(t, carry):
-            for s in (1, 2, 3):
-                j = t - (4 - s)
+        def x_rows(s):
+            return pl.ds((S - 1 - s) * 2 * XP, 2 * XP + (32 if s == 0 else 0))
+
+        def x_copy(s, m):
+            rows = x_rows(s)
+            at = 3 * s + m
+            return remote(sx.at[m, rows], rx.at[x, rows], r_s.at[at], r_r.at[at], x_peers[m])
+
+        def x_fill(ref, s, p, angles):
+            first = (S - 1 - s) * 2 * XP
+            for h in range(2):
+                rows = pl.ds(pl.multiple_of(s * W + p * XP, 64), XP)
+                ref[pl.ds(first + h * XP, XP)] = acc[h, rows].astype(BF16)
+            if s == 0:
+                ref[pl.ds(first + 2 * XP, 32)] = angles
+
+        def x_begin(s, angles=None):
+            for m in range(3):
+                x_fill(sx.at[m], s, flip(x, m + 1), angles)
+                x_copy(s, m).start()
+            x_fill(rx.at[x], s, x, angles)
+
+        def one_loop(t, carry):
+            def at_chunk(offset, last, body):
+                j = t - offset
 
                 @pl.when((j >= 0) & (j < n))
-                def _(s=s, j=j):
-                    back(s, j)
+                def _():
+                    body(j)
+
+                for s in last:
+
+                    @pl.when(j == n - 1)
+                    def _(s=s):
+                        x_begin(s)
+
+            at_chunk(LAG + 11, (1,), lambda j: back(1, j))
+            at_chunk(LAG + 10, (2,), lambda j: back(2, j))
+            at_chunk(LAG + 8, (3,), lambda j: back(3, j))
+            at_chunk(LAG + 5, (), lambda j: carry_on(3, n + j, 1))
+            at_chunk(LAG + 3, (), lambda j: carry_on(2, n + j, 1))
+            at_chunk(LAG + 1, (), lambda j: carry_on(1, n + j, 1))
+            at_chunk(8, (), lambda j: carry_on(3, j, 0))
+            at_chunk(5, (), lambda j: carry_on(2, j, 0))
+            at_chunk(2, (), lambda j: carry_on(1, j, 0))
+
+            @pl.when(t == 6)
+            def _():
+                weight_copy(0).wait_recv()
+                for step in (1, 2, 3):
+                    weight_copy(step).start()
+
+            @pl.when(t == 8)
+            def _():
+                for step in (1, 2, 3):
+                    weight_copy(step).wait_recv()
+                for step in (4, 5, 6):
+                    weight_copy(step).start()
+
+            @pl.when(t == LAG)
+            def _():
+                angle_copy().wait_recv()
+                twiddle(1, ang2[...])
+                for step in (4, 5, 6):
+                    weight_copy(step).wait_recv()
 
             @pl.when(t < n)
             def _():
-                turn(t)
-
+                own_copy(t).wait()
+                start(t, 0)
+
+            def begin(j):
+                vec_copy(j).wait_recv()
+
+                @pl.when(j + WINDOW < n)
+                def _():
+                    vec_copy(j + WINDOW).start()
+
+                start(n + j, 1)
+
+            at_chunk(LAG, (), begin)
+            at_chunk(LAG + 2, (), send_codes)
+            at_chunk(LAG + AHEAD, (4,), turn)
             return carry
 
-        lax.fori_loop(0, n + 3, backward, 0)
+        lax.fori_loop(0, n + LAG + 11, one_loop, 0)
 
         turned = []
         for h in range(2):
@@ -358,80 +414,73 @@
             turned.append(jnp.concatenate(parts, axis=0).astype(BF16))
         angles = jnp.concatenate(turned, axis=0)
 
-        def fill_x(ref, p):
+        def z_copy(stage, m):
+            at = 3 * (S + stage) + m
+            piece = pl.ds(pl.multiple_of(ii * ZS, 16), ZS)
+            source, target, peer = (
+                (sz.at[m], rz.at[ii], i_peers[m]),
+                (sk.at[m], rk.at[kk], k_peers[m]),
+                (gx.at[x, piece], gx.at[x, piece], i_peers[m]),
+                (gx.at[x], gx.at[x], x_peers[m]),
+            )[stage]
+            return remote(source, target, r_s.at[at], r_r.at[at], peer)
+
+        def total(ref):
+            return (ref[0].astype(F32) + ref[1].astype(F32)) + (
+                ref[2].astype(F32) + ref[3].astype(F32)
+            )
+
+        def z_fill(ref, p):
             for h in range(2):
-                ref[pl.ds(h * XS, XS)] = acc[h, pl.ds(pl.multiple_of(p * XS, 64), XS)].astype(BF16)
-            ref[pl.ds(2 * XS, 32)] = angles
-
-        def x_copy(m):
-            return remote(sx.at[m], rx.at[x], r_s.at[m], r_r.at[m], x_peers[m])
-
-        def i_copy(m):
-            return remote(sz.at[m], rz.at[ii], r_s.at[3 + m], r_r.at[3 + m], i_peers[m])
-
-        def k_copy(m):
-            return remote(sk.at[m], rk.at[kk], r_s.at[6 + m], r_r.at[6 + m], k_peers[m])
-
-        def gi_copy(m):
-            rows = pl.ds(pl.multiple_of(ii * ZS, 16), ZS)
-            return remote(
-                gx.at[x, rows], gx.at[x, rows], r_s.at[9 + m], r_r.at[9 + m], i_peers[m]
-            )
-
-        def gx_copy(m):
-            return remote(gx.at[x], gx.at[x], r_s.at[12 + m], r_r.at[12 + m], x_peers[m])
-
-        for m in range(3):
-            fill_x(sx.at[m], flip(x, m + 1))
-            x_copy(m).start()
-        fill_x(rx.at[x], x)
-        for m in range(3):
-            x_copy(m).wait_recv()
-        sxs[...] = (rx[0].astype(F32) + rx[1].astype(F32)) + (rx[2].astype(F32) + rx[3].astype(F32))
-
-        def fill_z(ref, p):
-            for h in range(2):
-                ref[pl.ds(h * ZS, ZS)] = sxs[
-                    pl.ds(pl.multiple_of(h * XS + p * ZS, 16), ZS)
-                ].astype(BF16)
+                for s in range(S):
+                    first = (S - 1 - s) * 2 * XP + h * XP
+                    rows = pl.ds(pl.multiple_of(first + p * ZP, 16), ZP)
+                    ref[pl.ds((h * S + s) * ZP, ZP)] = sxs[rows].astype(BF16)
             ref[pl.ds(2 * ZS, 32)] = sxs[pl.ds(2 * XS, 32)].astype(BF16)
 
-        for m in range(3):
-            fill_z(sz.at[m], flip(ii, m + 1))
-            i_copy(m).start()
-        fill_z(rz.at[ii], ii)
-        for m in range(3):
-            i_copy(m).wait_recv()
-        szs[...] = (rz[0].astype(F32) + rz[1].astype(F32)) + (rz[2].astype(F32) + rz[3].astype(F32))
-
-        def fill_k(ref, h):
+        def k_fill(ref, h):
             ref[pl.ds(0, ZS)] = szs[pl.ds(h * ZS, ZS)].astype(BF16)
             ref[pl.ds(ZS, 16)] = szs[pl.ds(2 * ZS + h * 16, 16)].astype(BF16)
 
-        for m in range(3):
-            fill_k(sk.at[m], 0 if m == 0 else 1)
-            k_copy(m).start()
-        fill_k(rk.at[kk], 0)
-        for m in range(3):
-            k_copy(m).wait_recv()
-        final = (rk[0].astype(F32) + rk[1].astype(F32)) + (rk[2].astype(F32) + rk[3].astype(F32))
+        x_begin(0, angles)
+        for s in reversed(range(S)):
+            for m in range(3):
+                x_copy(s, m).wait_recv()
+        sxs[...] = total(rx)
+        for m in range(3):
+            z_fill(sz.at[m], flip(ii, m + 1))
+            z_copy(0, m).start()
+        z_fill(rz.at[ii], ii)
+        for m in range(3):
+            z_copy(0, m).wait_recv()
+        szs[...] = total(rz)
+        for m in range(3):
+            k_fill(sk.at[m], 0 if m == 0 else 1)
+            z_copy(1, m).start()
+        k_fill(rk.at[kk], 0)
+        for m in range(3):
+            z_copy(1, m).wait_recv()
+        final = total(rk)
+        gx[x, pl.ds(pl.multiple_of(ii * ZS, 16), ZS)] = final[:ZS].astype(BF16)
+        for m in range(3):
+            z_copy(2, m).start()
         ang_o[...] = final[ZS:]
-        gx[x, pl.ds(pl.multiple_of(ii * ZS, 16), ZS)] = final[:ZS].astype(BF16)
-
-        for m in range(3):
-            gi_copy(m).start()
-        for m in range(3):
-            gi_copy(m).wait_recv()
-        for m in range(3):
-            gx_copy(m).start()
-        for m in range(3):
-            gx_copy(m).wait_recv()
+        for m in range(3):
+            z_copy(2, m).wait_recv()
+        for m in range(3):
+            z_copy(3, m).start()
+        for m in range(3):
+            z_copy(3, m).wait_recv()
         for p in range(4):
-            grad_o[pl.ds(p * XS, XS)] = gx[p].astype(F32)
-
-        for step in range(4):
+            for q in range(4):
+                for s in range(S):
+                    grad_o[pl.ds(s * W + p * XP + q * ZP, ZP)] = gx[
+                        p, pl.ds(q * ZS + s * ZP, ZP)
+                    ].astype(F32)
+
+        for step in range(7):
             weight_copy(step).wait_send()
-        trig_copy().wait_send()
+        angle_copy().wait_send()
 
         def drain(j, carry):
             vec_copy(j).wait_send()
@@ -444,8 +493,10 @@
 
         lax.fori_loop(0, n, drain, 0)
         for m in range(3):
-            for copy in (x_copy, i_copy, k_copy, gi_copy, gx_copy):
-                copy(m).wait_send()
+            for s in range(S):
+                x_copy(s, m).wait_send()
+            for stage in range(4):
+                z_copy(stage, m).wait_send()
 
     return kernel, n
 
@@ -467,6 +518,7 @@
         pltpu.VMEM((n, R, W), BF16),
         pltpu.VMEM((2, S * W, BLOCK), BF16),
         pltpu.VMEM((2, 16, W), F32),
+        pltpu.VMEM((S, W), F32),
         pltpu.VMEM((16, BLOCK), F32),
         pltpu.VMEM((num_rows // 2, BLOCK), F32),
         pltpu.VMEM((2, S * W, BLOCK), F32),
@@ -482,8 +534,9 @@
         pltpu.VMEM((4, ZS + 16, BLOCK), BF16),
         pltpu.VMEM((4, XS, BLOCK), BF16),
         dma((n,)),
-        dma((4,)), dma((4,)), dma((1,)), dma((1,)), dma((n,)), dma((n,)), dma((n,)), dma((n,)),
-        dma((3, 2 * n)), dma((3, 2 * n)), dma((3, n)), dma((3, n)), dma((15,)), dma((15,)),
+        dma((7,)), dma((7,)), dma((1,)), dma((1,)), dma((n,)), dma((n,)), dma((n,)), dma((n,)),
+        dma((3, 2 * n)), dma((3, 2 * n)), dma((3, n)), dma((3, n)),
+        dma((27,)), dma((27,)),
     ]
     return pl.pallas_call(
         kernel,

time: 200 us -> 171 us (0.85)
  the two profiles are of different devices: /device:TPU:1 before, /device:TPU:8 now
where the time goes in v2:
time: 171 us
  Pallas kernels  167 us (98%)
  other arithmetic  2.89 us (2%)
    pallas_call x1, Pallas kernels, gradients(): pl.pallas_call(kernel, name='butterfly', out_shape=(jax.ShapeDtypeStruct(...  167 us

profile of v2, /device:TPU:8, one launch (start us, length us, event | category | flops | bytes accessed | tf_op | source)
XLA Modules:
  0.0 170.5 jit_solution(7207712176261574015)
XLA Ops:
  0.6 0.0 copy-start
  0.6 167.0 %butterfly.1 = (f32[1280,128]{1,0:T(8,128)}, f32[16,128]{1,0:T(8,128)}) custom-call(bf16[1664,256]{1,0:T(8,128)(2,1)} %vec.1, s32[1664,256]{1,0:T(8,128)} %codes.1, f32[1280,128]{1,0:T(8,128)} %bitcast.5, f32[5,256]{1,0:T(8,128)} %ang.1, s32[13,128]{1,0:T(8,128)} %bitcast.6, f32[16]{0:T(128)} %tab.1), custom_call_target="tpu_custom_call" | custom-call | tf_op jit(solution)/shard_map/butterfly/pallas_call | solution.py:541
  167.6 0.0 copy-start.1
  167.6 0.0 copy-start.2
  167.6 0.0 copy-done
  167.6 2.3 %rsqrt_multiply_fusion = (f32[5,256,128]{2,1,0:T(8,128)}, f32[5,256,128]{2,1,0:T(8,128)}) fusion(f32[5,256,128]{2,1,0:T(8,128)} %bitcast.4, f32[5,256,128]{2,1,0:T(8,128)S(1)} %copy-done), kind=kLoop, calls=%fused_computation.2 | loop fusion | flops 819200 | bytes 2621440 | tf_op jit(solution)/shard_map/div | solution.py:569
  169.9 0.0 copy-done.1
  169.9 0.0 copy-done.2
  169.9 0.6 rsqrt_multiply_fusion.1
  (1 shorter events, 0.0 us)
Async XLA Ops:
  0.6 167.0 %copy-start = (f32[5,256,128]{2,1,0:T(8,128)S(1)}, f32[5,256,128]{2,1,0:T(8,128)}, u32[]{:S(2)}) copy-start(f32[5,256,128]{2,1,0:T(8,128)} %param.14) | copy-start | bytes 1966084
  167.6 2.3 %copy-start.1 = (f32[16,128]{1,0:T(8,128)S(1)}, f32[16,128]{1,0:T(8,128)}, u32[]{:S(2)}) copy-start(f32[16,128]{1,0:T(8,128)} %get-tuple-element.7) | copy-start | bytes 24580
  167.6 2.3 %copy-start.2 = (f32[5,256]{1,0:T(8,128)S(1)}, f32[5,256]{1,0:T(8,128)}, u32[]{:S(2)}) copy-start(f32[5,256]{1,0:T(8,128)} %param.15) | copy-start | bytes 15364

commit v3 on v2

--- a/solution.py
+++ b/solution.py
@@ -18,7 +18,7 @@
 ZP = XP // 4
 AHEAD = 6
 WINDOW = 4
-LAG = 9
+LAG = 11
 MESH = pl.DeviceIdType.MESH
 F32 = jnp.float32
 BF16 = jnp.bfloat16

time: 171 us -> 170 us (level)
  no operation moved by 1% of the time
where the time goes in v3:
time: 170 us
  Pallas kernels  166 us (98%)
  other arithmetic  2.89 us (2%)
    pallas_call x1, Pallas kernels, gradients(): pl.pallas_call(kernel, name='butterfly', out_shape=(jax.ShapeDtypeStruct(...  166 us

profile of v3, /device:TPU:8, one launch (start us, length us, event | category | flops | bytes accessed | tf_op | source)
XLA Modules:
  0.0 169.8 jit_solution(11148994283320916665)
XLA Ops:
  0.6 0.0 copy-start
  0.6 166.2 %butterfly.1 = (f32[1280,128]{1,0:T(8,128)}, f32[16,128]{1,0:T(8,128)}) custom-call(bf16[1664,256]{1,0:T(8,128)(2,1)} %vec.1, s32[1664,256]{1,0:T(8,128)} %codes.1, f32[1280,128]{1,0:T(8,128)} %bitcast.5, f32[5,256]{1,0:T(8,128)} %ang.1, s32[13,128]{1,0:T(8,128)} %bitcast.6, f32[16]{0:T(128)} %tab.1), custom_call_target="tpu_custom_call" | custom-call | tf_op jit(solution)/shard_map/butterfly/pallas_call | solution.py:541
  166.9 0.0 copy-start.1
  166.9 0.0 copy-start.2
  166.9 0.0 copy-done
  166.9 2.3 %rsqrt_multiply_fusion = (f32[5,256,128]{2,1,0:T(8,128)}, f32[5,256,128]{2,1,0:T(8,128)}) fusion(f32[5,256,128]{2,1,0:T(8,128)} %bitcast.4, f32[5,256,128]{2,1,0:T(8,128)S(1)} %copy-done), kind=kLoop, calls=%fused_computation.2 | loop fusion | flops 819200 | bytes 2621440 | tf_op jit(solution)/shard_map/div | solution.py:569
  169.2 0.0 copy-done.1
  169.2 0.0 copy-done.2
  169.2 0.6 rsqrt_multiply_fusion.1
  (1 shorter events, 0.0 us)
Async XLA Ops:
  0.6 166.3 %copy-start = (f32[5,256,128]{2,1,0:T(8,128)S(1)}, f32[5,256,128]{2,1,0:T(8,128)}, u32[]{:S(2)}) copy-start(f32[5,256,128]{2,1,0:T(8,128)} %param.14) | copy-start | bytes 1966084
  166.9 2.3 %copy-start.1 = (f32[16,128]{1,0:T(8,128)S(1)}, f32[16,128]{1,0:T(8,128)}, u32[]{:S(2)}) copy-start(f32[16,128]{1,0:T(8,128)} %get-tuple-element.7) | copy-start | bytes 24580
  166.9 2.3 %copy-start.2 = (f32[5,256]{1,0:T(8,128)S(1)}, f32[5,256]{1,0:T(8,128)}, u32[]{:S(2)}) copy-start(f32[5,256]{1,0:T(8,128)} %param.15) | copy-start | bytes 15364
